TPU v7x, 128 devices: a whole 4x4x4 slice. The times are simulated.
128 devices in a mesh: row: 8 (over z, core), col: 16 (over y, x).
Axes of the slice: x: 4, y: 4, z: 4, core: 2. Of those that a mesh axis runs over, the one named last changes fastest.
Arguments:
- emb: bfloat16 [524288, 512], P(('row', 'col')), may hold values from -6 to 6
- tiles: bfloat16 [2048, 4, 256, 256], P(('row', 'col')), may hold values from -0.375 to 0.375
- msg_src: int32 [2048, 4], P(('row', 'col')), may hold values from 0 to 15
- msg_dst: int32 [2048, 4], P(('row', 'col')), may hold values from 0 to 16, as said below
- msg_count: int32 [2048, 4], P(('row', 'col')), may hold values from 1 to 256
- weight: bfloat16 [512, 512], replicated, may hold values from -0.25 to 0.25
- docs: bfloat16 [512, 512], P('row'), may hold values from -0.059814453 to 0.099609375
- doc_labels: int32 [512, 8], replicated, may hold values from 0 to 524287
Outputs:
- hidden: bfloat16 [524288, 512], P(('row', 'col'))
- grad_docs: float32 [512, 512], P('row')
- grad_weight: float32 [512, 512], replicated
Inputs may be any that keep to these rules, and one draw needn't show every extreme that they name: For each sending device and each column of its row, the used slots (msg_dst below 16) come first and 16 marks an unused slot. In every row of devices some column receives all 4 slots used from every sender of that row.
All inputs are finite; a program needn't handle non-finite values.
Results may differ from a plain program's by a relative error of at most 0.0052.
Values may be sent and summed in bfloat16 or wider, within the bound.
No kernel may reach another device: no remote copies, remote signals or barrier semaphores. Data moves between devices by JAX's collectives and lax.ppermute only.
A program may use at most 192 MiB of HBM per device.

v0:
```python
import jax
import jax.numpy as jnp
from jax import lax
from jax.sharding import PartitionSpec as P


def per_device(emb, tiles, msg_src, msg_dst, msg_count, weight, docs, doc_labels):
    n_col = lax.axis_size("col")
    n_row = lax.axis_size("row")
    label_dev, width = emb.shape
    blk = tiles.shape[-1]
    cap = tiles.shape[1]
    blk_dev = label_dev // blk
    labels_total = float(label_dev * n_row * n_col)
    pos_count = doc_labels.shape[1]
    own_blocks = emb.reshape(blk_dev, blk, width)
    picked = own_blocks[msg_src]
    messages = jnp.einsum(
        "pqij,pqjd->pqid", tiles, picked, preferred_element_type=jnp.float32
    ).astype(jnp.bfloat16)
    received, dst_seen, cnt_seen = (
        lax.all_to_all(messages, "col", split_axis=0, concat_axis=0, tiled=True),
        lax.all_to_all(
            msg_dst.astype(jnp.bfloat16), "col", split_axis=0, concat_axis=0, tiled=True
        ),
        lax.all_to_all(
            msg_count.astype(jnp.bfloat16), "col", split_axis=0, concat_axis=0, tiled=True
        ),
    )
    slots_all = n_col * cap
    block_ids = jnp.arange(blk_dev, dtype=jnp.float32)
    hot = (dst_seen.astype(jnp.float32).reshape(1, slots_all) == block_ids[:, None]).astype(
        jnp.float32
    )
    weighted = hot * cnt_seen.astype(jnp.float32).reshape(1, slots_all)
    total = jnp.dot(
        weighted.astype(jnp.bfloat16),
        received.reshape(slots_all, blk * width),
        preferred_element_type=jnp.float32,
    ).reshape(blk_dev, blk, width)
    total = total + float(blk) * own_blocks.astype(jnp.float32)
    denom = float(blk) + jnp.sum(weighted, axis=1)
    agg = (total / denom[:, None, None]).astype(jnp.bfloat16).reshape(label_dev, width)
    pre = jnp.dot(agg, weight, preferred_element_type=jnp.float32)
    hidden = jax.nn.silu(pre).astype(jnp.bfloat16)
    device = lax.axis_index("row") * n_col + lax.axis_index("col")
    label_ids = device * label_dev + jnp.arange(label_dev, dtype=jnp.int32)
    piece = lax.all_gather(docs, "row", axis=0, tiled=True)
    scores = jnp.einsum("nd,ld->nl", piece, hidden, preferred_element_type=jnp.float32)
    positive = doc_labels[:, 0:1] == label_ids[None, :]
    for which in range(1, pos_count):
        positive = positive | (doc_labels[:, which : which + 1] == label_ids[None, :])
    prob = jax.nn.sigmoid(scores)
    dscore = jnp.where(positive, (prob - 1.0) / float(pos_count), prob / labels_total).astype(
        jnp.bfloat16
    )
    rows_grad = jnp.dot(dscore, hidden, preferred_element_type=jnp.float32)
    dhid = jnp.einsum("nl,nd->ld", dscore, piece, preferred_element_type=jnp.float32)
    doc_grad = rows_grad
    dhid, doc_grad = (dhid, doc_grad)
    sig = jax.nn.sigmoid(pre)
    dpre = (dhid * sig * (1.0 + pre * (1.0 - sig))).astype(jnp.bfloat16)
    weight_part = jnp.einsum("la,lb->ab", agg, dpre, preferred_element_type=jnp.float32)
    grad_weight = lax.psum(weight_part, ("row", "col"))
    row_share = lax.psum_scatter(doc_grad, "row", scatter_dimension=0, tiled=True)
    grad_docs = lax.psum(row_share, "col")
    return (hidden, grad_docs, grad_weight)


def solution(mesh):
    in_specs = (
        P(("row", "col"), None),
        P(("row", "col"), None, None, None),
        P(("row", "col"), None),
        P(("row", "col"), None),
        P(("row", "col"), None),
        P(),
        P("row", None),
        P(),
    )
    out_specs = (P(("row", "col"), None), P("row", None), P())
    return jax.shard_map(
        per_device, mesh=mesh, in_specs=in_specs, out_specs=out_specs, check_vma=False
    )
```

profile of v0, /device:TPU:0, one launch (start us, length us, event | category | flops | bytes accessed | tf_op | source)
XLA Modules:
  0.0 621.5 jit_solution(9641399624754386184)
XLA Ops:
  8.0 0.7 convert_bitcast_fusion.2
  8.8 0.7 copy.23
  9.5 7.1 %all-to-all-start = ((bf16[16,1,4]{2,1,0:T(2,128)(2,1)}), bf16[16,1,4]{2,1,0:T(2,128)(2,1)S(1)}, u32[]{:S(2)}, u32[]{:S(2)}) async-start(bf16[16,1,4]{2,1,0:T(2,128)(2,1)} %copy.23), calls=%async_computation | async-start | bytes 16384 | tf_op jit(solution)/shard_map/all_to_all | solution.py:23
  16.6 0.7 convert_bitcast_fusion.1
  17.3 0.7 copy.24
  18.0 0.7 compare_select_fusion
  18.7 0.1 copy.25
  18.8 0.1 reshape.51
  18.9 9.8 %gather_fusion = bf16[64,256,512]{2,1,0:T(8,128)(2,1)} fusion(bf16[16,256,512]{2,1,0:T(8,128)(2,1)} %bitcast.53, s32[1024]{0:T(1024)S(1)} %pad_clamp_fusion), kind=kCustom, calls=%fused_computation | custom fusion | bytes 33554688 | tf_op jit(solution)/shard_map/gather | solution.py:17
  28.7 7.2 %all-to-all-start.1 = ((bf16[16,1,4]{2,1,0:T(2,128)(2,1)}), bf16[16,1,4]{2,1,0:T(2,128)(2,1)S(1)}, u32[]{:S(2)}, u32[]{:S(2)}) async-start(bf16[16,1,4]{2,1,0:T(2,128)(2,1)} %copy.24), calls=%async_computation.1 | async-start | bytes 16384 | tf_op jit(solution)/shard_map/all_to_all | solution.py:26
  35.9 19.3 %convert_bitcast_fusion = bf16[16,4,256,512]{2,3,1,0:T(8,128)(2,1)} fusion(bf16[16,4,256,512]{3,2,1,0:T(8,128)(2,1)} %bitcast.52, bf16[16,4,256,256]{3,2,1,0:T(8,128)(2,1)} %param.9), kind=kOutput, calls=%fused_computation.4 | convolution fusion | flops 4303355904 | bytes 41943040 | tf_op jit(solution)/shard_map/pqij,pqjd->pqid/dot_general | solution.py:18
  55.2 7.4 %all-to-all-start.2 = ((bf16[16,4,256,512]{2,3,1,0:T(8,128)(2,1)}), bf16[16,4,256,512]{2,3,1,0:T(8,128)(2,1)}, u32[]{:S(2)}, u32[]{:S(2)}) async-start(bf16[16,4,256,512]{2,3,1,0:T(8,128)(2,1)} %convert_bitcast_fusion), calls=%async_computation.2 | async-start | bytes 33554432 | tf_op jit(solution)/shard_map/all_to_all | solution.py:22
  62.7 14.5 %all_gather.3 = bf16[512,512]{1,0:T(8,128)(2,1)S(1)} all-gather(bf16[64,512]{1,0:T(8,128)(2,1)S(1)} %copy-done.5), channel_id=1, replica_groups=mesh['row'=8,'col'=16] {'row'}, dimensions={0}, use_global_device_ids=true | all-gather | bytes 589824 | tf_op jit(solution)/shard_map/all_gather | solution.py:48
  77.2 0.1 reshape.47
  77.4 0.1 reshape.48
  77.5 0.1 select_reduce_fusion
  77.6 228.8 %all-to-all-done.2 = bf16[16,4,256,512]{2,3,1,0:T(8,128)(2,1)} async-done(((bf16[16,4,256,512]{2,3,1,0:T(8,128)(2,1)}), bf16[16,4,256,512]{2,3,1,0:T(8,128)(2,1)}, u32[]{:S(2)}, u32[]{:S(2)}) %all-to-all-start.2) | async-done | bytes 16777248 | tf_op jit(solution)/shard_map/all_to_all | solution.py:22
  306.4 24.3 %copy.33 = bf16[8,8,256,512]{3,1,2,0:T(8,128)(2,1)} copy(bf16[8,8,256,512]{2,3,1,0:T(8,128)(2,1)} %bitcast.36) | data formatting | bytes 33554432
  330.8 9.2 %divide_convert_fusion = bf16[16,256,512]{2,0,1:T(8,128)(2,1)S(1)} fusion(bf16[16,256,512]{2,1,0:T(8,128)(2,1)} %bitcast.54, f32[16]{0:T(128)S(1)} %broadcast_add_fusion, f32[64]{0:T(128)S(1)} %reshape.48, f32[64]{0:T(128)S(1)} %reshape.47, bf16[8,8,256,512]{3,1,2,0:T(8,128)(2,1)} %copy.33), kind=kOutput, calls=%fused_computation.10 | convolution fusion | flops 278923264 | bytes 25166400 | tf_op jit(solution)/shard_map/dot_general | solution.py:36
  339.9 2.4 copy.30
  342.4 5.7 multiply_convert_fusion.1
  348.0 10.1 %fusion.3 = bf16[512,4096]{0,1:T(8,128)(2,1)S(1)} fusion(bf16[4096,512]{1,0:T(8,128)(2,1)S(1)} %get-tuple-element.13, bf16[512,512]{1,0:T(8,128)(2,1)S(1)} %all_gather.3, s32[512]{0:T(512)S(1)} %bitcast.63, s32[512]{0:T(512)S(1)} %bitcast.64, s32[512]{0:T(512)S(1)} %bitcast.58, s32[512]{0:T(512)S(1)} %bitcast.59, s32[512]{0:T(512)S(1)} %bitcast.60, ...), kind=kOutput, calls=%fused_computation.6 | convolution fusion | flops 2195718144 | bytes 8945664 | tf_op jit(solution)/shard_map/nd,ld->nl/dot_general | solution.py:49
  358.1 1.9 copy-done.3
  360.1 3.3 fusion.15
  363.4 0.3 all-reduce.5.cloned.1.call-start
  363.7 12.6 %fusion.6 = f32[512,512]{1,0:T(8,128)} fusion(bf16[4096,512]{1,0:T(8,128)(2,1)} %bitcast.56, f32[4096,512]{1,0:T(8,128)} %get-tuple-element.12, bf16[512,4096]{0,1:T(8,128)(2,1)} %copy-done.3, bf16[512,512]{1,0:T(8,128)(2,1)S(1)} %all_gather.3), kind=kOutput, calls=%fused_computation.11 | convolution fusion | flops 4313841664 | bytes 18350080 | tf_op jit(solution)/shard_map/la,lb->ab/dot_general | solution.py:63
  376.3 0.0 all-reduce.3.cloned.1.call-start
  376.4 22.1 %reduce-scatter.2.cloned.1.call-done = f32[64,512]{1,0:T(8,128)} async-done(((f32[512,512]{1,0:T(8,128)}), f32[64,512]{1,0:T(8,128)}) %reduce-scatter.2.cloned.1.call-update) | async-done | bytes 131088 | tf_op jit(solution)/shard_map/reduce_scatter | solution.py:65
  398.5 127.1 %all-reduce.5.cloned.1.call-done = f32[512,512]{1,0:T(8,128)} async-done(((f32[512,512]{1,0:T(8,128)}), f32[512,512]{1,0:T(8,128)}) %all-reduce.5.cloned.1.call-update) | async-done | bytes 1048592 | tf_op jit(solution)/shard_map/psum | solution.py:64
  525.6 84.6 %all-reduce.3.cloned.1.call-done = f32[64,512]{1,0:T(8,128)} async-done(((f32[64,512]{1,0:T(8,128)}), f32[64,512]{1,0:T(8,128)}) %all-reduce.3.cloned.1.call-update) | async-done | bytes 131088 | tf_op jit(solution)/shard_map/psum | solution.py:66
  610.2 1.6 copy.44
  611.8 2.3 copy.45
  (25 shorter events, 0.2 us)
Async XLA Ops:
  8.0 334.4 %copy-start = (bf16[512,512]{1,0:T(8,128)(2,1)S(1)}, bf16[512,512]{1,0:T(8,128)(2,1)}, u32[]{:S(2)}) copy-start(bf16[512,512]{1,0:T(8,128)(2,1)} %param.13) | copy-start | bytes 1572868
  9.5 19.2 %all-to-all-start = ((bf16[16,1,4]{2,1,0:T(2,128)(2,1)}), bf16[16,1,4]{2,1,0:T(2,128)(2,1)S(1)}, u32[]{:S(2)}, u32[]{:S(2)}) async-start(bf16[16,1,4]{2,1,0:T(2,128)(2,1)} %copy.23), calls=%async_computation | async-start | bytes 16384 | tf_op jit(solution)/shard_map/all_to_all | solution.py:23
  28.7 26.5 %all-to-all-start.1 = ((bf16[16,1,4]{2,1,0:T(2,128)(2,1)}), bf16[16,1,4]{2,1,0:T(2,128)(2,1)S(1)}, u32[]{:S(2)}, u32[]{:S(2)}) async-start(bf16[16,1,4]{2,1,0:T(2,128)(2,1)} %copy.24), calls=%async_computation.1 | async-start | bytes 16384 | tf_op jit(solution)/shard_map/all_to_all | solution.py:26
  55.2 7.5 %copy-start.6 = (s32[512,8]{0,1:T(8,128)S(1)}, s32[512,8]{0,1:T(8,128)}, u32[]{:S(2)}) copy-start(s32[512,8]{0,1:T(8,128)} %param.15) | copy-start | bytes 49156
  55.2 7.5 %copy-start.5 = (bf16[64,512]{1,0:T(8,128)(2,1)S(1)}, bf16[64,512]{1,0:T(8,128)(2,1)}, u32[]{:S(2)}) copy-start(bf16[64,512]{1,0:T(8,128)(2,1)} %param.14) | copy-start | bytes 196612
  55.2 251.3 %all-to-all-start.2 = ((bf16[16,4,256,512]{2,3,1,0:T(8,128)(2,1)}), bf16[16,4,256,512]{2,3,1,0:T(8,128)(2,1)}, u32[]{:S(2)}, u32[]{:S(2)}) async-start(bf16[16,4,256,512]{2,3,1,0:T(8,128)(2,1)} %convert_bitcast_fusion), calls=%async_computation.2 | async-start | bytes 33554432 | tf_op jit(solution)/shard_map/all_to_all | solution.py:22
  62.6 335.9 %reduce-scatter.2.cloned.1.call-start = ((), (), s32[]{:S(2)}) async-start(), calls=%async_computation.4 | async-start | bytes 1179648 | tf_op jit(solution)/shard_map/reduce_scatter | solution.py:65
  342.3 5.7 copy-start.4
  348.0 10.1 %copy-start.2 = (bf16[4096,512]{1,0:T(8,128)(2,1)}, bf16[4096,512]{1,0:T(8,128)(2,1)S(1)}, u32[]{:S(2)}) copy-start(bf16[4096,512]{1,0:T(8,128)(2,1)S(1)} %get-tuple-element.13) | copy-start | bytes 12582916
  358.1 1.9 copy-start.3
  363.4 162.2 %all-reduce.5.cloned.1.call-start = ((), (), s32[]{:S(2)}) async-start(), calls=%async_computation.6 | async-start | bytes 2097152 | tf_op jit(solution)/shard_map/psum | solution.py:64
  363.7 250.3 %copy-start.1 = (bf16[512,512]{1,0:T(8,128)(2,1)S(1)}, bf16[512,512]{1,0:T(8,128)(2,1)}, u32[]{:S(2)}) copy-start(bf16[512,512]{1,0:T(8,128)(2,1)} %param.13) | copy-start | bytes 1572868
  376.3 233.9 %all-reduce.3.cloned.1.call-start = ((), (), s32[]{:S(2)}) async-start(), calls=%async_computation.5 | async-start | bytes 262144 | tf_op jit(solution)/shard_map/psum | solution.py:66
Sparse Core Ops, SparseCore 0:
  363.5 34.9 reduce-scatter.1
Sparse Core Ops, SparseCore 1:
  376.4 149.2 all-reduce.4
  528.7 81.4 all-reduce.2
where the time goes:
time: 623 us; the launch traced here: 621 us
  waiting for transfers between devices  463 us (74%)
  matrix products  60.1 us (10%)
  local copies, waits for them, and re-layouts  44.1 us (7%)
  starting transfers between devices  22.1 us (4%)
  between operations  15.7 us (3%)
  blocking collectives  14.5 us (2%)
    all_to_all x1, waiting for transfers between devices, per_device(): lax.all_to_all(messages, 'col', split_axis=0, concat_axis=0, tiled=True)  229 us
    psum x1, waiting for transfers between devices, per_device(): grad_weight = lax.psum(weight_part, ('row', 'col'))  127 us
    psum x1, waiting for transfers between devices, per_device(): grad_docs = lax.psum(row_share, 'col')  84.6 us
    unnamed x17, local copies, waits for them, and re-layouts  30.1 us
    reduce_scatter x1, waiting for transfers between devices, per_device(): lax.psum_scatter(doc_grad, 'row', scatter_dimension=0, tiled=True)  22.1 us
    dot_general x1, matrix products, per_device(): jnp.einsum('pqij,pqjd->pqid', tiles, picked, preferred_element_type=jnp.f...  19.3 us
    all_gather x1, blocking collectives, per_device(): piece = lax.all_gather(docs, 'row', axis=0, tiled=True)  14.5 us
    dot_general x1, matrix products, per_device(): jnp.einsum('la,lb->ab', agg, dpre, preferred_element_type=jnp.float32)  12.6 us
  transfers between devices with their start and end apart: 6, of which 4 were waited for; matrix products, arithmetic and copies ran while one was open for 7% of the time, Pallas kernels for 0%

commit v1 on v0

v1 whole, which is shorter than its diff:
```python
import jax
import jax.numpy as jnp
from jax import lax
from jax.experimental import pallas as pl
from jax.experimental.pallas import tpu as pltpu
from jax.sharding import PartitionSpec as P

BF = jnp.bfloat16
F32 = jnp.float32
CHUNK_ROWS = (64, 64, 64, 64)
STEP_ROWS = 32


def message_kernel(src_ref, emb_ref, tile_ref, out_ref):
    p = pl.program_id(0)
    for q in range(tile_ref.shape[1]):
        block = emb_ref[src_ref[p, q]]
        out_ref[0, q] = jnp.dot(
            tile_ref[0, q], block, preferred_element_type=F32
        ).astype(BF)


def messages_of(src, blocks, tiles, row, rows):
    n_peer, cap, blk, _ = tiles.shape
    n_blk, _, width = blocks.shape
    at = row // rows
    return pl.pallas_call(
        message_kernel,
        grid_spec=pltpu.PrefetchScalarGridSpec(
            num_scalar_prefetch=1,
            grid=(n_peer,),
            in_specs=[
                pl.BlockSpec((n_blk, blk, width), lambda p, s: (0, 0, 0),
                             pipeline_mode=pl.Buffered(1)),
                pl.BlockSpec((1, cap, rows, blk), lambda p, s: (p, 0, at, 0)),
            ],
            out_specs=pl.BlockSpec((1, cap, rows, width), lambda p, s: (p, 0, 0, 0)),
        ),
        out_shape=jax.ShapeDtypeStruct((n_peer, cap, rows, width), BF),
        name="messages",
    )(src, blocks, tiles)


def head_kernel(first, blk, labels_total, pos_count,
                dst_ref, cnt_ref, inv_ref, recv_ref, emb_ref, pos_ref, w_ref, docs_ref,
                *rest):
    if first:
        hid_ref, gd_ref, gw_ref, acc_ref, agg_ref, ds_ref = rest
    else:
        gd_in, gw_in, _, hid_ref, gd_ref, gw_ref, acc_ref, agg_ref, ds_ref = rest
    step = pl.program_id(0)

    @pl.when(step == 0)
    def _():
        if first:
            gd_ref[...] = jnp.zeros_like(gd_ref)
            gw_ref[...] = jnp.zeros_like(gw_ref)
        else:
            gd_ref[...] = gd_in[...]
            gw_ref[...] = gw_in[...]

    n_blk, rows, width = emb_ref.shape
    own = float(blk)
    for b in range(n_blk):
        acc_ref[b] = own * emb_ref[b].astype(F32)
    n_slot = recv_ref.shape[0]

    def add(s, carry):
        d = dst_ref[s]

        @pl.when(d < n_blk)
        def _():
            acc_ref[d] = acc_ref[d] + cnt_ref[s] * recv_ref[s].astype(F32)
        return carry

    lax.fori_loop(0, n_slot, add, 0)
    for b in range(n_blk):
        agg_ref[b * rows:(b + 1) * rows, :] = (acc_ref[b] * inv_ref[b]).astype(BF)
    agg = agg_ref[...]
    pre = jnp.dot(agg, w_ref[...], preferred_element_type=F32)
    sig = 1.0 / (1.0 + jnp.exp(-pre))
    hid = (pre * sig).astype(BF)
    for b in range(n_blk):
        hid_ref[b] = hid[b * rows:(b + 1) * rows, :]
    scores = lax.dot_general(hid, docs_ref[...], (((1,), (1,)), ((), ())),
                             preferred_element_type=F32)
    prob = 1.0 / (1.0 + jnp.exp(-scores))
    for b in range(n_blk):
        part = prob[b * rows:(b + 1) * rows, :]
        ds_ref[b * rows:(b + 1) * rows, :] = jnp.where(
            pos_ref[b].astype(F32) > 0.5, (part - 1.0) * (1.0 / pos_count), part * (1.0 / labels_total)
        ).astype(BF)
    ds = ds_ref[...]
    gd_ref[...] += lax.dot_general(ds, hid, (((0,), (0,)), ((), ())),
                                   preferred_element_type=F32)
    dhid = jnp.dot(ds, docs_ref[...], preferred_element_type=F32)
    dpre = (dhid * sig * (1.0 + pre * (1.0 - sig))).astype(BF)
    gw_ref[...] += lax.dot_general(agg, dpre, (((0,), (0,)), ((), ())),
                                   preferred_element_type=F32)


def head(dst, cnt, inv, recv, blocks, positive, weight, docs, carry, row, rows,
         labels_total, pos_count):
    n_blk, blk, width = blocks.shape
    n_slot = recv.shape[0]
    step_rows = min(STEP_ROWS, rows)
    steps = rows // step_rows
    at = row // step_rows
    n_doc = docs.shape[0]
    first = carry is None
    smem = pl.BlockSpec(memory_space=pltpu.SMEM)
    full = lambda a: pl.BlockSpec(a, lambda i: (0, 0), pipeline_mode=pl.Buffered(1))
    rowed = lambda n: pl.BlockSpec((n_blk, step_rows, n), lambda i: (0, at + i, 0))
    in_specs = [
        smem, smem, smem,
        pl.BlockSpec((n_slot, step_rows, width), lambda i: (0, i, 0)),
        rowed(width), rowed(n_doc), full(weight.shape), full(docs.shape),
    ]
    args = [dst, cnt, inv, recv, blocks, positive, weight, docs]
    aliases = {}
    if not first:
        hid, gd, gw = carry
        in_specs += [full(gd.shape), full(gw.shape), pl.BlockSpec(memory_space=pl.ANY)]
        aliases = {len(args) + 2: 0}
        args += [gd, gw, hid]

    def body(*refs):
        head_kernel(first, blk, labels_total, pos_count, *refs)

    return pl.pallas_call(
        body,
        grid=(steps,),
        in_specs=in_specs,
        out_specs=[rowed(width),
                   pl.BlockSpec((n_doc, width), lambda i: (0, 0)),
                   pl.BlockSpec((width, width), lambda i: (0, 0))],
        out_shape=[jax.ShapeDtypeStruct(blocks.shape, BF),
                   jax.ShapeDtypeStruct((n_doc, width), F32),
                   jax.ShapeDtypeStruct((width, width), F32)],
        scratch_shapes=[pltpu.VMEM((n_blk, step_rows, width), F32),
                        pltpu.VMEM((n_blk * step_rows, width), BF),
                        pltpu.VMEM((n_blk * step_rows, n_doc), BF)],
        input_output_aliases=aliases,
        compiler_params=pltpu.CompilerParams(vmem_limit_bytes=48 << 20),
        name="head",
    )(*args)


def swap(x, axis):
    return lax.all_to_all(x, axis, split_axis=0, concat_axis=0, tiled=True)


def spread(x, axis, n):
    return swap(jnp.broadcast_to(x[None], (n,) + x.shape), axis)


def per_device(emb, tiles, msg_src, msg_dst, msg_count, weight, docs, doc_labels):
    n_col = lax.axis_size("col")
    n_row = lax.axis_size("row")
    label_dev, width = emb.shape
    n_peer, cap, blk, _ = tiles.shape
    blk_dev = label_dev // blk
    labels_total = float(label_dev * n_row * n_col)
    pos_count = doc_labels.shape[1]
    n_doc = docs.shape[0] * n_row
    blocks = emb.reshape(blk_dev, blk, width)

    starts = [sum(CHUNK_ROWS[:k]) for k in range(len(CHUNK_ROWS))]
    received = []
    sent = []
    for row, rows in zip(starts, CHUNK_ROWS):
        out = messages_of(msg_src, blocks, tiles, row, rows)
        sent.append(out)
        received.append(swap(out, "col").reshape(n_peer * cap, rows, width))

    table = swap(jnp.concatenate([msg_dst, msg_count], axis=1), "col")
    dst = table[:, :cap].reshape(-1)
    cnt = table[:, cap:].reshape(-1).astype(F32)
    hot = dst[None, :] == jnp.arange(blk_dev, dtype=jnp.int32)[:, None]
    inv = 1.0 / (float(blk) + jnp.sum(jnp.where(hot, cnt[None, :], 0.0), axis=1))

    all_docs = spread(docs, "row", n_row).reshape(n_doc, width)
    device = lax.axis_index("row") * n_col + lax.axis_index("col")
    label_ids = device * label_dev + jnp.arange(label_dev, dtype=jnp.int32)
    positive = jnp.any(
        label_ids[:, None, None] == doc_labels.T[None, :, :], axis=1
    ).astype(BF).reshape(blk_dev, blk, n_doc)

    carry = None
    for k, (row, rows) in enumerate(zip(starts, CHUNK_ROWS)):
        carry = head(dst, cnt, inv, received[k], blocks, positive, weight, all_docs, carry,
                     row, rows, labels_total, float(pos_count))
    hidden, gd, gw = carry

    both = jnp.concatenate([gd, gw], axis=1).astype(BF)
    share = n_doc // n_col
    part = swap(both.reshape(n_col, share, 2 * width), "col")
    part = jnp.sum(part.astype(F32), axis=0).astype(BF)
    part = spread(part, "row", n_row)
    part = jnp.sum(part.astype(F32), axis=0).astype(BF)
    whole = spread(part, "col", n_col).reshape(n_doc, 2 * width)
    mine = lax.dynamic_slice_in_dim(
        whole[:, :width], lax.axis_index("row") * docs.shape[0], docs.shape[0], 0
    )
    return (hidden.reshape(label_dev, width), mine.astype(F32), whole[:, width:].astype(F32))


def solution(mesh):
    in_specs = (
        P(("row", "col"), None),
        P(("row", "col"), None, None, None),
        P(("row", "col"), None),
        P(("row", "col"), None),
        P(("row", "col"), None),
        P(),
        P("row", None),
        P(),
    )
    out_specs = (P(("row", "col"), None), P("row", None), P())
    return jax.shard_map(
        per_device, mesh=mesh, in_specs=in_specs, out_specs=out_specs, check_vma=False
    )
```

time: 623 us -> 374 us (0.60)
  waiting for transfers between devices: 463 us -> 165 us
  Pallas kernels: 0 us -> 92.8 us
  matrix products: 60.1 us -> 0 us
  local copies, waits for them, and re-layouts: 44.1 us -> 4.68 us
  blocking collectives: 14.5 us -> 48.8 us
  other arithmetic: 2.3 us -> 32.4 us
  between operations: 15.7 us -> 0.78 us
    psum x2 -> x0, waiting for transfers between devices: 212 us -> none  [the longest x1 127 us: per_device(): grad_weight = lax.psum(weight_part, ('row', 'col'))]
    pallas_call x0 -> x8, Pallas kernels: none -> 92.8 us  [the longest x4 55.8 us: messages_of(): pl.pallas_call(message_kernel, grid_spec=pltpu.PrefetchScalarGridSpec(num...]
    all_to_all x3 -> x6, waiting for transfers between devices: 229 us -> 165 us  [swap(): return lax.all_to_all(x, axis, split_axis=0, concat_axis=0, tiled=True)]
    dot_general x6 -> x0, matrix products: 60.1 us -> none  [the longest x1 19.3 us: per_device(): jnp.einsum('pqij,pqjd->pqid', tiles, picked, preferred_element_type=jnp.f...]
    all_to_all x0 -> x3, blocking collectives: none -> 48.8 us  [swap(): return lax.all_to_all(x, axis, split_axis=0, concat_axis=0, tiled=True)]
    unnamed x17 -> x5, local copies, waits for them, and re-layouts: 30.1 us -> 1.36 us
    reduce_or x0 -> x1, other arithmetic: none -> 26.3 us  [per_device(): jnp.any(label_ids[:, None, None] == doc_labels.T[None, :, :], axis=1)]
    reduce_scatter x1 -> x0, waiting for transfers between devices: 22.1 us -> none  [per_device(): lax.psum_scatter(doc_grad, 'row', scatter_dimension=0, tiled=True)]
  transfers between devices with their start and end apart: 6 -> 6, of which waited for: 4 -> 5; matrix products, arithmetic and copies ran while one was open for 7% -> 8% of each run, Pallas kernels for 0% -> 22%
where the time goes in v1:
time: 374 us; the launch traced here: 372 us
  waiting for transfers between devices  165 us (44%)
  Pallas kernels  92.8 us (25%)
  blocking collectives  48.8 us (13%)
  other arithmetic  32.4 us (9%)
  starting transfers between devices  27.7 us (7%)
  local copies, waits for them, and re-layouts  4.68 us (1%)
    all_to_all x6, waiting for transfers between devices, swap(): return lax.all_to_all(x, axis, split_axis=0, concat_axis=0, tiled=True)  165 us
    pallas_call x4, Pallas kernels, messages_of(): pl.pallas_call(message_kernel, grid_spec=pltpu.PrefetchScalarGridSpec(num...  55.8 us
    all_to_all x3, blocking collectives, swap(): return lax.all_to_all(x, axis, split_axis=0, concat_axis=0, tiled=True)  48.8 us
    pallas_call x4, Pallas kernels, head(): pl.pallas_call(body, grid=(steps,), in_specs=in_specs, out_specs=[rowed(w...  36.9 us
    all_to_all x6, starting transfers between devices, swap(): return lax.all_to_all(x, axis, split_axis=0, concat_axis=0, tiled=True)  27.7 us
    reduce_or x1, other arithmetic, per_device(): jnp.any(label_ids[:, None, None] == doc_labels.T[None, :, :], axis=1)  26.3 us
  transfers between devices with their start and end apart: 6, of which 5 were waited for; matrix products, arithmetic and copies ran while one was open for 8% of the time, Pallas kernels for 22%

profile of v1, /device:TPU:0, one launch (start us, length us, event | category | flops | bytes accessed | tf_op | source)
XLA Modules:
  0.0 372.4 jit_solution(4085619231131802472)
XLA Ops:
  0.6 0.7 add_bitcast_fusion
  1.4 14.5 %all_to_all.52 = s32[16,1,8]{2,1,0:T(1,128)S(1)} all-to-all(s32[16,1,8]{2,1,0:T(1,128)S(1)} %copy.34), channel_id=1, replica_groups=mesh['row'=8,'col'=16] {'col'}, dimensions={0} | all-to-all | bytes 1024 | tf_op jit(solution)/shard_map/all_to_all | solution.py:150
  15.9 1.7 broadcast_in_dim.20
  17.6 5.3 %all-to-all-start.2 = ((bf16[8,64,512]{2,1,0:T(8,128)(2,1)}), bf16[8,64,512]{2,1,0:T(8,128)(2,1)S(1)}, u32[]{:S(2)}, u32[]{:S(2)}) async-start(bf16[8,64,512]{2,1,0:T(8,128)(2,1)} %broadcast_in_dim.20), calls=%async_computation.2 | async-start | bytes 1048576 | tf_op jit(solution)/shard_map/all_to_all | solution.py:150
  22.9 1.4 copy.38.src_ref
  24.3 13.9 %messages.7 = bf16[16,4,64,512]{3,2,1,0:T(8,128)(2,1)} custom-call(s32[16,4]{1,0:T(8,128)} %copy.38.src_ref, bf16[16,256,512]{2,1,0:T(8,128)(2,1)} %bitcast.19, bf16[16,4,256,256]{3,2,1,0:T(8,128)(2,1)} %tile_ref.7), custom_call_target="tpu_custom_call" | custom-call | tf_op jit(solution)/shard_map/messages/pallas_call | solution.py:27
  38.2 4.5 %all-to-all-start.5 = ((bf16[16,4,64,512]{3,2,1,0:T(8,128)(2,1)}), bf16[16,4,64,512]{3,2,1,0:T(8,128)(2,1)}, u32[]{:S(2)}, u32[]{:S(2)}) async-start(bf16[16,4,64,512]{3,2,1,0:T(8,128)(2,1)} %messages.7), calls=%async_computation.5 | async-start | bytes 8388608 | tf_op jit(solution)/shard_map/all_to_all | solution.py:150
  42.8 14.0 %messages.6 = bf16[16,4,64,512]{3,2,1,0:T(8,128)(2,1)} custom-call(s32[16,4]{1,0:T(8,128)} %copy.38.src_ref, bf16[16,256,512]{2,1,0:T(8,128)(2,1)} %bitcast.20, bf16[16,4,256,256]{3,2,1,0:T(8,128)(2,1)} %tile_ref.7), custom_call_target="tpu_custom_call" | custom-call | tf_op jit(solution)/shard_map/messages/pallas_call | solution.py:27
  56.8 51.4 %all-to-all-done.5 = bf16[16,4,64,512]{3,2,1,0:T(8,128)(2,1)} async-done(((bf16[16,4,64,512]{3,2,1,0:T(8,128)(2,1)}), bf16[16,4,64,512]{3,2,1,0:T(8,128)(2,1)}, u32[]{:S(2)}, u32[]{:S(2)}) %all-to-all-start.5) | async-done | bytes 4194336 | tf_op jit(solution)/shard_map/all_to_all | solution.py:150
  108.2 4.5 %all-to-all-start.4 = ((bf16[16,4,64,512]{3,2,1,0:T(8,128)(2,1)}), bf16[16,4,64,512]{3,2,1,0:T(8,128)(2,1)}, u32[]{:S(2)}, u32[]{:S(2)}) async-start(bf16[16,4,64,512]{3,2,1,0:T(8,128)(2,1)} %messages.6), calls=%async_computation.4 | async-start | bytes 8388608 | tf_op jit(solution)/shard_map/all_to_all | solution.py:150
  112.7 14.0 %messages.5 = bf16[16,4,64,512]{3,2,1,0:T(8,128)(2,1)} custom-call(s32[16,4]{1,0:T(8,128)} %copy.38.src_ref, bf16[16,256,512]{2,1,0:T(8,128)(2,1)} %bitcast.21, bf16[16,4,256,256]{3,2,1,0:T(8,128)(2,1)} %tile_ref.7), custom_call_target="tpu_custom_call" | custom-call | tf_op jit(solution)/shard_map/messages/pallas_call | solution.py:27
  126.7 49.3 %all-to-all-done.4 = bf16[16,4,64,512]{3,2,1,0:T(8,128)(2,1)} async-done(((bf16[16,4,64,512]{3,2,1,0:T(8,128)(2,1)}), bf16[16,4,64,512]{3,2,1,0:T(8,128)(2,1)}, u32[]{:S(2)}, u32[]{:S(2)}) %all-to-all-start.4) | async-done | bytes 4194336 | tf_op jit(solution)/shard_map/all_to_all | solution.py:150
  176.0 4.9 %all-to-all-start.3 = ((bf16[16,4,64,512]{3,2,1,0:T(8,128)(2,1)}), bf16[16,4,64,512]{3,2,1,0:T(8,128)(2,1)}, u32[]{:S(2)}, u32[]{:S(2)}) async-start(bf16[16,4,64,512]{3,2,1,0:T(8,128)(2,1)} %messages.5), calls=%async_computation.3 | async-start | bytes 8388608 | tf_op jit(solution)/shard_map/all_to_all | solution.py:150
  181.0 13.9 %messages.4 = bf16[16,4,64,512]{3,2,1,0:T(8,128)(2,1)} custom-call(s32[16,4]{1,0:T(8,128)} %copy.38.src_ref, bf16[16,256,512]{2,1,0:T(8,128)(2,1)} %bitcast.22, bf16[16,4,256,256]{3,2,1,0:T(8,128)(2,1)} %tile_ref.7), custom_call_target="tpu_custom_call" | custom-call | tf_op jit(solution)/shard_map/messages/pallas_call | solution.py:27
  194.9 46.7 %all-to-all-done.3 = bf16[16,4,64,512]{3,2,1,0:T(8,128)(2,1)} async-done(((bf16[16,4,64,512]{3,2,1,0:T(8,128)(2,1)}), bf16[16,4,64,512]{3,2,1,0:T(8,128)(2,1)}, u32[]{:S(2)}, u32[]{:S(2)}) %all-to-all-start.3) | async-done | bytes 4194336 | tf_op jit(solution)/shard_map/all_to_all | solution.py:150
  241.6 4.7 %all-to-all-start.1 = ((bf16[16,4,64,512]{3,2,1,0:T(8,128)(2,1)}), bf16[16,4,64,512]{3,2,1,0:T(8,128)(2,1)}, u32[]{:S(2)}, u32[]{:S(2)}) async-start(bf16[16,4,64,512]{3,2,1,0:T(8,128)(2,1)} %messages.4), calls=%async_computation.1 | async-start | bytes 8388608 | tf_op jit(solution)/shard_map/all_to_all | solution.py:150
  246.3 26.3 %compare_reduce_fusion = pred[4096,512]{1,0:T(8,128)(4,1)S(1)} fusion(s32[8,512]{1,0:T(8,128)S(1)} %bitcast.35, s32[4096]{0:T(1024)S(1)} %iota_add_fusion), kind=kLoop, calls=%fused_computation | loop fusion | flops 31457280 | bytes 2129920 | tf_op jit(solution)/shard_map/reduce_or | solution.py:185
  272.7 2.9 convert_element_type.30
  276.2 9.2 %head.4 = (bf16[16,256,512]{2,1,0:T(8,128)(2,1)}, f32[512,512]{1,0:T(8,128)S(1)}, f32[512,512]{1,0:T(8,128)S(1)}) custom-call(s32[64]{0:T(128)S(1)} %reshape.60.refs_0_, f32[64]{0:T(128)S(1)} %convert_element_type.25.refs_1_, f32[16]{0:T(128)S(1)} %add_divide_fusion.refs_2_, bf16[64,64,512]{2,1,0:T(8,128)(2,1)} %bitcast.9.refs_3_, ...), custom_call_target="tpu_custom_call" | custom-call | tf_op jit(solution)/shard_map/head/pallas_call | solution.py:130
  285.3 9.2 %head.5 = (bf16[16,256,512]{2,1,0:T(8,128)(2,1)}, f32[512,512]{1,0:T(8,128)S(1)}, f32[512,512]{1,0:T(8,128)S(1)}) custom-call(s32[64]{0:T(128)S(1)} %reshape.60.refs_0_, f32[64]{0:T(128)S(1)} %convert_element_type.25.refs_1_, f32[16]{0:T(128)S(1)} %add_divide_fusion.refs_2_, bf16[64,64,512]{2,1,0:T(8,128)(2,1)} %bitcast.8.refs_3_, ...), custom_call_target="tpu_custom_call", output_to_operand_aliasing={{0}: (10, {})} | custom-call | tf_op jit(solution)/shard_map/head/pallas_call | solution.py:130
  294.6 9.3 %head.6 = (bf16[16,256,512]{2,1,0:T(8,128)(2,1)}, f32[512,512]{1,0:T(8,128)S(1)}, f32[512,512]{1,0:T(8,128)S(1)}) custom-call(s32[64]{0:T(128)S(1)} %reshape.60.refs_0_, f32[64]{0:T(128)S(1)} %convert_element_type.25.refs_1_, f32[16]{0:T(128)S(1)} %add_divide_fusion.refs_2_, bf16[64,64,512]{2,1,0:T(8,128)(2,1)} %bitcast.7.refs_3_, ...), custom_call_target="tpu_custom_call", output_to_operand_aliasing={{0}: (10, {})} | custom-call | tf_op jit(solution)/shard_map/head/pallas_call | solution.py:130
  303.9 0.3 all-to-all-done.1
  304.1 9.2 %head.7 = (bf16[16,256,512]{2,1,0:T(8,128)(2,1)}, f32[512,512]{1,0:T(8,128)S(1)}, f32[512,512]{1,0:T(8,128)S(1)}) custom-call(s32[64]{0:T(128)S(1)} %reshape.60.refs_0_, f32[64]{0:T(128)S(1)} %convert_element_type.25.refs_1_, f32[16]{0:T(128)S(1)} %add_divide_fusion.refs_2_, bf16[64,64,512]{2,1,0:T(8,128)(2,1)} %bitcast.3.refs_3_, ...), custom_call_target="tpu_custom_call", output_to_operand_aliasing={{0}: (10, {})} | custom-call | tf_op jit(solution)/shard_map/head/pallas_call | solution.py:130
  313.5 0.1 pad_maximum_fusion
  313.6 21.6 %all_to_all.53 = bf16[16,32,1024]{2,1,0:T(8,128)(2,1)S(1)} all-to-all(bf16[16,32,1024]{2,1,0:T(8,128)(2,1)S(1)} %pad_maximum_fusion), channel_id=1, replica_groups=mesh['row'=8,'col'=16] {'col'}, dimensions={0} | all-to-all | bytes 2097152 | tf_op jit(solution)/shard_map/all_to_all | solution.py:150
  335.2 0.2 reduce_sum.34
  335.5 12.8 %all_to_all.54 = bf16[8,32,1024]{2,1,0:T(8,128)(2,1)S(1)} all-to-all(bf16[8,32,1024]{2,1,0:T(8,128)(2,1)S(1)} %broadcast_in_dim.21), channel_id=1, replica_groups=mesh['row'=8,'col'=16] {'row'}, dimensions={0} | all-to-all | bytes 1048576 | tf_op jit(solution)/shard_map/all_to_all | solution.py:150
  348.3 1.1 broadcast_in_dim.22
  349.4 3.7 all-to-all-start.8
  353.1 17.5 %all-to-all-done.8 = bf16[16,32,1024]{2,1,0:T(8,128)(2,1)S(1)} async-done(((bf16[16,32,1024]{2,1,0:T(8,128)(2,1)}), bf16[16,32,1024]{2,1,0:T(8,128)(2,1)S(1)}, u32[]{:S(2)}, u32[]{:S(2)}) %all-to-all-start.8) | async-done | bytes 1048608 | tf_op jit(solution)/shard_map/all_to_all | solution.py:150
  370.6 1.1 slice_convert_fusion
  371.7 0.7 dynamic-slice_convert_fusion
  (19 shorter events, 0.9 us)
Async XLA Ops:
  17.6 20.6 %all-to-all-start.2 = ((bf16[8,64,512]{2,1,0:T(8,128)(2,1)}), bf16[8,64,512]{2,1,0:T(8,128)(2,1)S(1)}, u32[]{:S(2)}, u32[]{:S(2)}) async-start(bf16[8,64,512]{2,1,0:T(8,128)(2,1)} %broadcast_in_dim.20), calls=%async_computation.2 | async-start | bytes 1048576 | tf_op jit(solution)/shard_map/all_to_all | solution.py:150
  38.2 69.9 %all-to-all-start.5 = ((bf16[16,4,64,512]{3,2,1,0:T(8,128)(2,1)}), bf16[16,4,64,512]{3,2,1,0:T(8,128)(2,1)}, u32[]{:S(2)}, u32[]{:S(2)}) async-start(bf16[16,4,64,512]{3,2,1,0:T(8,128)(2,1)} %messages.7), calls=%async_computation.5 | async-start | bytes 8388608 | tf_op jit(solution)/shard_map/all_to_all | solution.py:150
  108.2 67.9 %all-to-all-start.4 = ((bf16[16,4,64,512]{3,2,1,0:T(8,128)(2,1)}), bf16[16,4,64,512]{3,2,1,0:T(8,128)(2,1)}, u32[]{:S(2)}, u32[]{:S(2)}) async-start(bf16[16,4,64,512]{3,2,1,0:T(8,128)(2,1)} %messages.6), calls=%async_computation.4 | async-start | bytes 8388608 | tf_op jit(solution)/shard_map/all_to_all | solution.py:150
  176.0 65.5 %all-to-all-start.3 = ((bf16[16,4,64,512]{3,2,1,0:T(8,128)(2,1)}), bf16[16,4,64,512]{3,2,1,0:T(8,128)(2,1)}, u32[]{:S(2)}, u32[]{:S(2)}) async-start(bf16[16,4,64,512]{3,2,1,0:T(8,128)(2,1)} %messages.5), calls=%async_computation.3 | async-start | bytes 8388608 | tf_op jit(solution)/shard_map/all_to_all | solution.py:150
  194.9 51.4 %copy-start.1 = (s32[512,8]{0,1:T(8,128)S(1)}, s32[512,8]{0,1:T(8,128)}, u32[]{:S(2)}) copy-start(s32[512,8]{0,1:T(8,128)} %param.15) | copy-start | bytes 49156
  241.6 62.6 %all-to-all-start.1 = ((bf16[16,4,64,512]{3,2,1,0:T(8,128)(2,1)}), bf16[16,4,64,512]{3,2,1,0:T(8,128)(2,1)}, u32[]{:S(2)}, u32[]{:S(2)}) async-start(bf16[16,4,64,512]{3,2,1,0:T(8,128)(2,1)} %messages.4), calls=%async_computation.1 | async-start | bytes 8388608 | tf_op jit(solution)/shard_map/all_to_all | solution.py:150
  246.3 29.8 %copy-start = (bf16[512,512]{1,0:T(8,128)(2,1)S(1)}, bf16[512,512]{1,0:T(8,128)(2,1)}, u32[]{:S(2)}) copy-start(bf16[512,512]{1,0:T(8,128)(2,1)} %refs_6_.7) | copy-start | bytes 1572868
  349.4 21.2 %all-to-all-start.8 = ((bf16[16,32,1024]{2,1,0:T(8,128)(2,1)}), bf16[16,32,1024]{2,1,0:T(8,128)(2,1)S(1)}, u32[]{:S(2)}, u32[]{:S(2)}) async-start(bf16[16,32,1024]{2,1,0:T(8,128)(2,1)} %broadcast_in_dim.22), calls=%async_computation.8 | async-start | bytes 2097152 | tf_op jit(solution)/shard_map/all_to_all | solution.py:150
